TPU v7x, 32 devices: a whole 2x2x4 slice. The times are simulated.
32 devices in a mesh: seq: 8 (over y, x, core), head: 4 (over z).
Axes of the slice: x: 2, y: 2, z: 4, core: 2. Of those that a mesh axis runs over, the one named last changes fastest.
Arguments:
- query_rows: bfloat16 [4096, 2048], P('seq', 'head'), may hold values from -6 to 6
- key_rows: bfloat16 [4096, 128], P('seq'), may hold values from -6 to 6
- value_rows: bfloat16 [4096, 128], P('seq'), may hold values from -6 to 6
- output_grad: bfloat16 [4096, 2048], P('seq', 'head'), may hold values from -0.59765625 to 0.59765625
- log_norm: float32 [16, 4096], P('head', 'seq'), may hold values from 0.5 to 3
- row_delta: float32 [16, 4096], P('head', 'seq'), may hold values from -5 to 5
- dispatch: int32 [8, 64], replicated, may hold values from 0 to 7, as said below
- listed_spans: int32 [8, 16], replicated, may hold values from 0 to 127, as said below
- range_start: int32 [8, 64], replicated, may hold values from 0 to 4088, as said below
Outputs:
- query_grad: bfloat16 [4096, 2048], P('seq', 'head')
- key_grad: float32 [128, 4096], P('head', 'seq')
- value_grad: float32 [128, 4096], P('head', 'seq')
Inputs may be any that keep to these rules, and one draw needn't show every extreme that they name: `dispatch`: entry [h, j] names the group of query span 64 * h + j. Every group holds exactly 64 spans, and each row gives at most 8 spans to any one group, a number that every row reaches. `listed_spans`: row g holds 16 distinct key spans for group g. At most 2 of them lie among the 16 key spans of one index of seq, and every row reaches that number. `range_start`: entry [h, j] is at most 8 * (64 * h + j).
All inputs are finite; a program needn't handle non-finite values.
Results may differ from a plain program's by a relative error of at most 0.0046.
Values may be sent and summed in bfloat16 or wider, within the bound.
A program may use at most 64 MiB of HBM per device.

v0:
```python
import math

import jax
import jax.numpy as jnp
from jax import lax
from jax.sharding import PartitionSpec as P

HD = 128
GROUP = 16
HQ_DEV = 4
SPAN = 8
KVCH = 32
NLIST = 16


HIGH = lax.Precision.HIGHEST


def passed_along(value, axis, by):
    length = lax.axis_size(axis)
    pairs = [(i, i + by) for i in range(length) if 0 <= i + by < length]
    return lax.ppermute(value, axis, pairs)


def earlier_same(labels):
    count = labels.shape[-1]
    same = labels[..., :, None] == labels[..., None, :]
    before = jnp.arange(count)[:, None] > jnp.arange(count)[None, :]
    return jnp.sum(same & before, axis=-1)


def one_hot(index, count):
    return (index[..., None] == jnp.arange(count, dtype=jnp.int32)).astype(jnp.float32)


def group_total(stacked, members, position, from_after):
    share = stacked.shape[1] // members

    def block(index):
        return lax.dynamic_slice_in_dim(stacked, index * share, share, 1)

    running = block((position + 1) % members)
    for step in range(1, members):
        running = from_after(running) + block((position + 1 + step) % members)
    return running


def local(
    query_rows,
    key_rows,
    value_rows,
    output_grad,
    log_norm,
    row_delta,
    dispatch,
    listed_spans,
    range_start,
):
    owners = lax.axis_size("seq")
    home_index = lax.axis_index("seq")
    head_index = lax.axis_index("head")
    spans = dispatch.shape[1]
    slot_count = max(1, spans // owners)
    kv_count = max(1, NLIST // owners)
    tok_dev = query_rows.shape[0]
    width = query_rows.shape[1]
    heads = width // HD
    blocks = tok_dev // KVCH
    members = GROUP // heads
    position = head_index % members
    kv_head = head_index * heads // GROUP
    score_scale = 1.0 / math.sqrt(HD)
    rank_all = earlier_same(dispatch)
    slot_all = dispatch * slot_count + rank_all
    to_slot = one_hot(slot_all[home_index], owners * slot_count)
    to_slot_bf = to_slot.astype(jnp.bfloat16)
    pick_bf = to_slot.T.astype(jnp.bfloat16)
    pick_float = to_slot.T

    def send_rows(rows):
        return (
            jnp.dot(pick_bf, rows.reshape(spans, -1), preferred_element_type=jnp.float32)
            .astype(jnp.bfloat16)
            .reshape(owners, slot_count * SPAN, -1)
        )

    def send_stats(stats):
        placed = jnp.dot(pick_float, stats.T.reshape(spans, SPAN * heads), precision=HIGH)
        return placed.reshape(owners, slot_count * SPAN, heads)

    list_home = listed_spans // blocks
    list_sub = listed_spans % blocks
    list_rank = earlier_same(list_home)
    mine = (list_home == home_index).astype(jnp.float32)
    rank_hot = one_hot(list_rank, kv_count) * mine[..., None]
    sub_hot = one_hot(list_sub, blocks)
    select = jnp.einsum("nir,nim->nrm", rank_hot, sub_hot, precision=HIGH).reshape(
        owners * kv_count, blocks
    )
    select_bf = select.astype(jnp.bfloat16)
    key_head = lax.dynamic_slice_in_dim(key_rows, kv_head * HD, HD, 1)
    value_head = lax.dynamic_slice_in_dim(value_rows, kv_head * HD, HD, 1)

    def send_blocks(rows):
        placed = jnp.dot(
            select_bf, rows.reshape(blocks, KVCH * HD), preferred_element_type=jnp.float32
        )
        return placed.astype(jnp.bfloat16).reshape(owners, kv_count * KVCH, HD)

    query_got, grad_got, key_got, value_got = (
        lax.all_to_all(send_rows(query_rows), "seq", split_axis=0, concat_axis=0, tiled=True),
        lax.all_to_all(send_rows(output_grad), "seq", split_axis=0, concat_axis=0, tiled=True),
        lax.all_to_all(send_blocks(key_head), "seq", split_axis=0, concat_axis=0, tiled=True),
        lax.all_to_all(send_blocks(value_head), "seq", split_axis=0, concat_axis=0, tiled=True),
    )
    norm_got, delta_got = (
        lax.all_to_all(send_stats(log_norm), "seq", split_axis=0, concat_axis=0, tiled=True),
        lax.all_to_all(send_stats(row_delta), "seq", split_axis=0, concat_axis=0, tiled=True),
    )
    live = (dispatch == home_index).reshape(-1)
    placement = jnp.cumsum(live.astype(jnp.int32)) - 1
    taken = live[:, None] & (placement[:, None] == jnp.arange(spans, dtype=jnp.int32)[None, :])
    source_slot = (jnp.arange(owners, dtype=jnp.int32)[:, None] * slot_count + rank_all).reshape(-1)
    compact = jnp.dot(
        taken.astype(jnp.float32).T, one_hot(source_slot, owners * slot_count), precision=HIGH
    )
    compact_bf = compact.astype(jnp.bfloat16)
    compact_back = compact.T.astype(jnp.bfloat16)
    flat_ids = jnp.arange(owners * spans, dtype=jnp.int32)
    span_ids = jnp.sum(jnp.where(taken, flat_ids[:, None], 0), axis=0)
    span_starts = jnp.sum(jnp.where(taken, range_start.reshape(-1)[:, None], 0), axis=0)

    def gather_rows(got):
        rows = jnp.dot(
            compact_bf, got.reshape(owners * slot_count, -1), preferred_element_type=jnp.float32
        )
        return rows.astype(jnp.bfloat16).reshape(spans * SPAN, heads, HD)

    def gather_stats(got):
        rows = jnp.dot(compact, got.reshape(owners * slot_count, SPAN * heads), precision=HIGH)
        return rows.reshape(spans * SPAN, heads).T

    query_mine = gather_rows(query_got)
    grad_mine = gather_rows(grad_got)
    norm_mine = gather_stats(norm_got)
    delta_mine = gather_stats(delta_got)
    my_list = listed_spans[home_index]
    kv_compact = one_hot(
        list_home[home_index] * kv_count + list_rank[home_index], owners * kv_count
    )
    kv_compact_bf = kv_compact.astype(jnp.bfloat16)

    def gather_blocks(got):
        rows = jnp.dot(
            kv_compact_bf,
            got.reshape(owners * kv_count, KVCH * HD),
            preferred_element_type=jnp.float32,
        )
        return rows.astype(jnp.bfloat16).reshape(NLIST * KVCH, HD)

    key_mine = gather_blocks(key_got)
    value_mine = gather_blocks(value_got)
    query_pos = (span_ids[:, None] * SPAN + jnp.arange(SPAN, dtype=jnp.int32)[None, :]).reshape(-1)
    key_pos = (my_list[:, None] * KVCH + jnp.arange(KVCH, dtype=jnp.int32)[None, :]).reshape(-1)
    lowest = jnp.repeat(span_starts, SPAN)
    allowed = (key_pos[None, :] <= query_pos[:, None]) & (key_pos[None, :] >= lowest[:, None])
    scores = (
        jnp.einsum("qhd,kd->hqk", query_mine, key_mine, preferred_element_type=jnp.float32)
        * score_scale
    )
    probs = jnp.where(allowed[None], jnp.exp(scores - norm_mine[:, :, None]), 0.0)
    dprobs = jnp.einsum("qhd,kd->hqk", grad_mine, value_mine, preferred_element_type=jnp.float32)
    dscores = probs * (dprobs - delta_mine[:, :, None])
    probs_bf = probs.astype(jnp.bfloat16)
    dscores_bf = dscores.astype(jnp.bfloat16)
    value_part = jnp.einsum("hqk,qhd->kd", probs_bf, grad_mine, preferred_element_type=jnp.float32)
    key_part = (
        jnp.einsum("hqk,qhd->kd", dscores_bf, query_mine, preferred_element_type=jnp.float32)
        * score_scale
    )
    query_part = (
        jnp.einsum("hqk,kd->qhd", dscores_bf, key_mine, preferred_element_type=jnp.float32)
        * score_scale
    )
    query_round = query_part.astype(jnp.bfloat16)
    query_send = jnp.dot(
        compact_back, query_round.reshape(spans, SPAN * width), preferred_element_type=jnp.float32
    )
    query_send = query_send.astype(jnp.bfloat16).reshape(owners, slot_count * SPAN, width)
    query_back = lax.all_to_all(query_send, "seq", split_axis=0, concat_axis=0, tiled=True)
    query_rows_out = jnp.dot(
        to_slot_bf,
        query_back.reshape(owners * slot_count, SPAN * width),
        preferred_element_type=jnp.float32,
    )
    query_out = query_rows_out.reshape(tok_dev, width).astype(jnp.bfloat16)

    def send_partial(part):
        rows = jnp.dot(kv_compact.T, part.reshape(NLIST, KVCH * HD), precision=HIGH)
        return rows.reshape(owners, kv_count * KVCH, HD)

    key_back, value_back = (
        lax.all_to_all(send_partial(key_part), "seq", split_axis=0, concat_axis=0, tiled=True),
        lax.all_to_all(send_partial(value_part), "seq", split_axis=0, concat_axis=0, tiled=True),
    )

    def home_rows(got):
        rows = jnp.dot(select.T, got.reshape(owners * kv_count, KVCH * HD), precision=HIGH)
        return rows.reshape(tok_dev, HD).T

    def after_home(running):
        nearby = passed_along(running, "head", -1)
        wrapped = passed_along(running, "head", GROUP // HQ_DEV - 1)
        return jnp.where(position == members - 1, wrapped, nearby)

    summed = group_total(
        jnp.stack([home_rows(key_back), home_rows(value_back)]), members, position, after_home
    )
    return (query_out, summed[0], summed[1])


def solution(mesh):
    placed = (
        P("seq", "head"),
        P("seq", None),
        P("seq", None),
        P("seq", "head"),
        P("head", "seq"),
        P("head", "seq"),
        P(),
        P(),
        P(),
    )
    return jax.shard_map(
        local,
        mesh=mesh,
        in_specs=placed,
        out_specs=(P("seq", "head"), P("head", "seq"), P("head", "seq")),
        check_vma=False,
    )
```

profile of v0, /device:TPU:0, one launch (start us, length us, event | category | flops | bytes accessed | tf_op | source)
XLA Modules:
  0.0 132.7 jit_solution(1162666161274121942)
XLA Ops:
  0.7 0.9 copy.59
  1.8 1.1 convert_reduce_fusion
  2.8 0.8 broadcast_add_fusion
  4.2 0.7 reshape.358
  4.9 5.2 %all-to-all-start.2 = ((f32[8,1,256]{2,1,0:T(1,128)}), f32[8,1,256]{2,1,0:T(1,128)S(1)}, u32[]{:S(2)}, u32[]{:S(2)}) async-start(f32[8,1,256]{2,1,0:T(1,128)} %reshape.358), calls=%async_computation.2 | async-start | bytes 16384 | tf_op jit(solution)/shard_map/all_to_all | solution.py:117
  10.1 0.7 fusion.66
  10.8 0.7 add_select_fusion.1
  11.5 0.7 compare_convert_fusion
  12.2 0.7 fusion.58
  13.6 1.3 reshape.315
  15.2 0.8 broadcast_in_dim.32
  16.6 1.3 reshape.327
  19.9 0.7 reshape.356
  20.6 4.2 %all-to-all-start.5 = ((f32[8,1,256]{2,1,0:T(1,128)}), f32[8,1,256]{2,1,0:T(1,128)S(1)}, u32[]{:S(2)}, u32[]{:S(2)}) async-start(f32[8,1,256]{2,1,0:T(1,128)} %reshape.356), calls=%async_computation.5 | async-start | bytes 16384 | tf_op jit(solution)/shard_map/all_to_all | solution.py:118
  25.0 0.7 reshape.312
  25.8 3.8 %all-to-all-done.5 = f32[8,1,256]{2,1,0:T(1,128)S(1)} async-done(((f32[8,1,256]{2,1,0:T(1,128)}), f32[8,1,256]{2,1,0:T(1,128)S(1)}, u32[]{:S(2)}, u32[]{:S(2)}) %all-to-all-start.5) | async-done | bytes 8224 | tf_op jit(solution)/shard_map/all_to_all | solution.py:118
  29.5 3.4 %all-to-all-start = ((bf16[8,64,128]{2,1,0:T(8,128)(2,1)}), bf16[8,64,128]{2,1,0:T(8,128)(2,1)S(1)}, u32[]{:S(2)}, u32[]{:S(2)}) async-start(bf16[8,64,128]{2,1,0:T(8,128)(2,1)} %reshape.312), calls=%async_computation | async-start | bytes 262144 | tf_op jit(solution)/shard_map/all_to_all | solution.py:113
  33.1 0.7 reshape.324
  33.9 4.5 %all-to-all-done = bf16[8,64,128]{2,1,0:T(8,128)(2,1)S(1)} async-done(((bf16[8,64,128]{2,1,0:T(8,128)(2,1)}), bf16[8,64,128]{2,1,0:T(8,128)(2,1)S(1)}, u32[]{:S(2)}, u32[]{:S(2)}) %all-to-all-start) | async-done | bytes 131104 | tf_op jit(solution)/shard_map/all_to_all | solution.py:113
  38.3 3.4 %all-to-all-start.3 = ((bf16[8,64,128]{2,1,0:T(8,128)(2,1)}), bf16[8,64,128]{2,1,0:T(8,128)(2,1)S(1)}, u32[]{:S(2)}, u32[]{:S(2)}) async-start(bf16[8,64,128]{2,1,0:T(8,128)(2,1)} %reshape.324), calls=%async_computation.3 | async-start | bytes 262144 | tf_op jit(solution)/shard_map/all_to_all | solution.py:114
  42.0 1.0 reshape.316
  43.0 1.0 reshape.328
  44.1 0.5 broadcast.164
  44.6 0.7 reduce.3
  45.7 1.5 %all-to-all-done.3 = bf16[8,64,128]{2,1,0:T(8,128)(2,1)S(1)} async-done(((bf16[8,64,128]{2,1,0:T(8,128)(2,1)}), bf16[8,64,128]{2,1,0:T(8,128)(2,1)S(1)}, u32[]{:S(2)}, u32[]{:S(2)}) %all-to-all-start.3) | async-done | bytes 131104 | tf_op jit(solution)/shard_map/all_to_all | solution.py:114
  47.1 3.5 %all-to-all-start.1 = ((bf16[8,64,512]{2,1,0:T(8,128)(2,1)}), bf16[8,64,512]{2,1,0:T(8,128)(2,1)S(1)}, u32[]{:S(2)}, u32[]{:S(2)}) async-start(bf16[8,64,512]{2,1,0:T(8,128)(2,1)} %reshape.316), calls=%async_computation.1 | async-start | bytes 1048576 | tf_op jit(solution)/shard_map/all_to_all | solution.py:111
  51.1 0.7 reduce.2
  52.9 0.7 reshape.314
  53.7 6.6 %all-to-all-done.1 = bf16[8,64,512]{2,1,0:T(8,128)(2,1)S(1)} async-done(((bf16[8,64,512]{2,1,0:T(8,128)(2,1)}), bf16[8,64,512]{2,1,0:T(8,128)(2,1)S(1)}, u32[]{:S(2)}, u32[]{:S(2)}) %all-to-all-start.1) | async-done | bytes 524320 | tf_op jit(solution)/shard_map/all_to_all | solution.py:111
  60.3 3.7 %all-to-all-start.4 = ((bf16[8,64,512]{2,1,0:T(8,128)(2,1)}), bf16[8,64,512]{2,1,0:T(8,128)(2,1)S(1)}, u32[]{:S(2)}, u32[]{:S(2)}) async-start(bf16[8,64,512]{2,1,0:T(8,128)(2,1)} %reshape.328), calls=%async_computation.4 | async-start | bytes 1048576 | tf_op jit(solution)/shard_map/all_to_all | solution.py:112
  64.2 0.7 reshape.349
  65.5 0.4 reshape.318
  65.8 7.6 %all-to-all-done.4 = bf16[8,64,512]{2,1,0:T(8,128)(2,1)S(1)} async-done(((bf16[8,64,512]{2,1,0:T(8,128)(2,1)}), bf16[8,64,512]{2,1,0:T(8,128)(2,1)S(1)}, u32[]{:S(2)}, u32[]{:S(2)}) %all-to-all-start.4) | async-done | bytes 524320 | tf_op jit(solution)/shard_map/all_to_all | solution.py:112
  74.0 0.4 reshape.330
  74.3 0.7 fusion.17
  75.1 0.9 fusion.10
  76.0 2.6 %fusion.1 = bf16[4,512,512]{1,2,0:T(8,128)(2,1)S(1)} fusion(f32[512,512,4]{1,0,2:T(8,128)S(1)} %fusion.17, bf16[512,128,1]{1,0,2:T(8,128)(2,1)S(1)} %copy-done.4, f32[4,512]{1,0:T(4,128)S(1)} %copy.71, f32[4,512]{1,0:T(4,128)S(1)} %copy.64, pred[512,512]{0,1:T(8,128)(4,1)} %copy-done.1, bf16[512,4,128]{2,1,0:T(4,128)(2,1)S(1)} %reshape.330), kind=kOutput, calls=%fused_computation.12 | convolution fusion | flops 274726912 | bytes 7225344 | tf_op jit(solution)/shard_map/qhd,kd->hqk/dot_general | solution.py:172
  78.6 0.7 fusion.13
  79.4 0.4 fusion.44
  79.8 0.7 reshape.340
  80.5 3.4 %all-to-all-start.7 = ((f32[8,64,128]{2,1,0:T(8,128)}), f32[8,64,128]{2,1,0:T(8,128)S(1)}, u32[]{:S(2)}, u32[]{:S(2)}) async-start(f32[8,64,128]{2,1,0:T(8,128)} %reshape.340), calls=%async_computation.7 | async-start | bytes 524288 | tf_op jit(solution)/shard_map/all_to_all | solution.py:203
  84.0 0.4 fusion.43
  84.4 0.7 reshape.344
  85.1 0.5 fusion.9
  85.9 0.4 reshape.335
  86.3 4.5 %all-to-all-done.7 = f32[8,64,128]{2,1,0:T(8,128)S(1)} async-done(((f32[8,64,128]{2,1,0:T(8,128)}), f32[8,64,128]{2,1,0:T(8,128)S(1)}, u32[]{:S(2)}, u32[]{:S(2)}) %all-to-all-start.7) | async-done | bytes 262176 | tf_op jit(solution)/shard_map/all_to_all | solution.py:203
  90.8 3.4 %all-to-all-start.8 = ((f32[8,64,128]{2,1,0:T(8,128)}), f32[8,64,128]{2,1,0:T(8,128)S(1)}, u32[]{:S(2)}, u32[]{:S(2)}) async-start(f32[8,64,128]{2,1,0:T(8,128)} %reshape.344), calls=%async_computation.8 | async-start | bytes 524288 | tf_op jit(solution)/shard_map/all_to_all | solution.py:204
  94.3 0.4 fusion.70
  94.9 6.2 %all-to-all-done.8 = f32[8,64,128]{2,1,0:T(8,128)S(1)} async-done(((f32[8,64,128]{2,1,0:T(8,128)}), f32[8,64,128]{2,1,0:T(8,128)S(1)}, u32[]{:S(2)}, u32[]{:S(2)}) %all-to-all-start.8) | async-done | bytes 262176 | tf_op jit(solution)/shard_map/all_to_all | solution.py:204
  101.1 0.4 fusion.71
  101.7 5.5 %collective-permute-start = (f32[2,32,512]{2,1,0:T(8,128)S(1)}, f32[2,32,512]{2,1,0:T(8,128)S(1)}, u32[]{:S(2)}, u32[]{:S(2)}) collective-permute-start(f32[2,32,512]{2,1,0:T(8,128)S(1)} %fusion.22), channel_id=1, source_target_pairs={{0,3},{4,7},{8,11},{12,15},{16,19},{20,23},{24,27},{28,31}} | collective-permute-start | bytes 393224 | tf_op jit(solution)/shard_map/ppermute | solution.py:22
  107.3 1.3 collective-permute-start.1
  108.9 1.0 reshape.336
  109.9 3.5 %all-to-all-start.6 = ((bf16[8,64,512]{2,1,0:T(8,128)(2,1)}), bf16[8,64,512]{2,1,0:T(8,128)(2,1)S(1)}, u32[]{:S(2)}, u32[]{:S(2)}) async-start(bf16[8,64,512]{2,1,0:T(8,128)(2,1)} %reshape.336), calls=%async_computation.6 | async-start | bytes 1048576 | tf_op jit(solution)/shard_map/all_to_all | solution.py:190
  113.5 0.7 collective-permute-done.1
  114.1 1.8 %collective-permute-start.2 = (f32[2,32,512]{2,1,0:T(8,128)S(1)}, f32[2,32,512]{2,1,0:T(8,128)S(1)}, u32[]{:S(2)}, u32[]{:S(2)}) collective-permute-start(f32[2,32,512]{2,1,0:T(8,128)S(1)} %fusion.24), channel_id=1, source_target_pairs={{0,3},{4,7},{8,11},{12,15},{16,19},{20,23},{24,27},{28,31}} | collective-permute-start | bytes 393224 | tf_op jit(solution)/shard_map/ppermute | solution.py:22
  115.9 1.3 collective-permute-start.3
  117.3 5.8 %all-to-all-done.6 = bf16[8,64,512]{2,1,0:T(8,128)(2,1)S(1)} async-done(((bf16[8,64,512]{2,1,0:T(8,128)(2,1)}), bf16[8,64,512]{2,1,0:T(8,128)(2,1)S(1)}, u32[]{:S(2)}, u32[]{:S(2)}) %all-to-all-start.6) | async-done | bytes 524320 | tf_op jit(solution)/shard_map/all_to_all | solution.py:190
  123.4 1.7 %collective-permute-start.4 = (f32[2,32,512]{2,1,0:T(8,128)S(1)}, f32[2,32,512]{2,1,0:T(8,128)S(1)}, u32[]{:S(2)}, u32[]{:S(2)}) collective-permute-start(f32[2,32,512]{2,1,0:T(8,128)S(1)} %fusion.26), channel_id=1, source_target_pairs={{0,3},{4,7},{8,11},{12,15},{16,19},{20,23},{24,27},{28,31}} | collective-permute-start | bytes 393224 | tf_op jit(solution)/shard_map/ppermute | solution.py:22
  125.1 1.3 collective-permute-start.5
  126.4 0.3 convolution_convert_fusion
  126.8 1.0 convert_element_type.122
  127.8 4.2 %collective-permute-done.5 = f32[2,32,512]{2,1,0:T(8,128)S(1)} collective-permute-done((f32[2,32,512]{2,1,0:T(8,128)S(1)}, f32[2,32,512]{2,1,0:T(8,128)S(1)}, u32[]{:S(2)}, u32[]{:S(2)}) %collective-permute-start.5) | collective-permute-done | bytes 131104 | tf_op jit(solution)/shard_map/ppermute | solution.py:22
  132.0 0.7 slice_bitcast_fusion
  (93 shorter events, 9.8 us)
Async XLA Ops:
  0.6 17.5 %copy-start.5 = (f32[4,512]{1,0:T(4,128)S(1)}, f32[4,512]{1,0:T(4,128)}, u32[]{:S(2)}) copy-start(f32[4,512]{1,0:T(4,128)} %param.14) | copy-start | bytes 24580
  0.6 18.9 %copy-start.2 = (bf16[512,128]{1,0:T(8,128)(2,1)S(1)}, bf16[512,128]{1,0:T(8,128)(2,1)}, u32[]{:S(2)}) copy-start(bf16[512,128]{1,0:T(8,128)(2,1)} %param.10) | copy-start | bytes 393220
  0.7 25.0 %copy-start.3 = (bf16[512,128]{1,0:T(8,128)(2,1)S(1)}, bf16[512,128]{1,0:T(8,128)(2,1)}, u32[]{:S(2)}) copy-start(bf16[512,128]{1,0:T(8,128)(2,1)} %param.11) | copy-start | bytes 393220
  4.9 15.7 %all-to-all-start.2 = ((f32[8,1,256]{2,1,0:T(1,128)}), f32[8,1,256]{2,1,0:T(1,128)S(1)}, u32[]{:S(2)}, u32[]{:S(2)}) async-start(f32[8,1,256]{2,1,0:T(1,128)} %reshape.358), calls=%async_computation.2 | async-start | bytes 16384 | tf_op jit(solution)/shard_map/all_to_all | solution.py:117
  19.3 55.7 %copy-start.1 = (pred[512,512]{0,1:T(8,128)(4,1)}, pred[512,512]{0,1:T(8,128)(4,1)S(1)}, u32[]{:S(2)}) copy-start(pred[512,512]{0,1:T(8,128)(4,1)S(1)} %compare_and_fusion) | copy-start | bytes 786436
  20.6 8.9 %all-to-all-start.5 = ((f32[8,1,256]{2,1,0:T(1,128)}), f32[8,1,256]{2,1,0:T(1,128)S(1)}, u32[]{:S(2)}, u32[]{:S(2)}) async-start(f32[8,1,256]{2,1,0:T(1,128)} %reshape.356), calls=%async_computation.5 | async-start | bytes 16384 | tf_op jit(solution)/shard_map/all_to_all | solution.py:118
  29.5 8.8 %all-to-all-start = ((bf16[8,64,128]{2,1,0:T(8,128)(2,1)}), bf16[8,64,128]{2,1,0:T(8,128)(2,1)S(1)}, u32[]{:S(2)}, u32[]{:S(2)}) async-start(bf16[8,64,128]{2,1,0:T(8,128)(2,1)} %reshape.312), calls=%async_computation | async-start | bytes 262144 | tf_op jit(solution)/shard_map/all_to_all | solution.py:113
  38.3 8.8 %all-to-all-start.3 = ((bf16[8,64,128]{2,1,0:T(8,128)(2,1)}), bf16[8,64,128]{2,1,0:T(8,128)(2,1)S(1)}, u32[]{:S(2)}, u32[]{:S(2)}) async-start(bf16[8,64,128]{2,1,0:T(8,128)(2,1)} %reshape.324), calls=%async_computation.3 | async-start | bytes 262144 | tf_op jit(solution)/shard_map/all_to_all | solution.py:114
  47.1 13.2 %all-to-all-start.1 = ((bf16[8,64,512]{2,1,0:T(8,128)(2,1)}), bf16[8,64,512]{2,1,0:T(8,128)(2,1)S(1)}, u32[]{:S(2)}, u32[]{:S(2)}) async-start(bf16[8,64,512]{2,1,0:T(8,128)(2,1)} %reshape.316), calls=%async_computation.1 | async-start | bytes 1048576 | tf_op jit(solution)/shard_map/all_to_all | solution.py:111
  60.3 13.1 %all-to-all-start.4 = ((bf16[8,64,512]{2,1,0:T(8,128)(2,1)}), bf16[8,64,512]{2,1,0:T(8,128)(2,1)S(1)}, u32[]{:S(2)}, u32[]{:S(2)}) async-start(bf16[8,64,512]{2,1,0:T(8,128)(2,1)} %reshape.328), calls=%async_computation.4 | async-start | bytes 1048576 | tf_op jit(solution)/shard_map/all_to_all | solution.py:112
  75.1 1.0 copy-start.4
  78.6 6.5 %copy-start = (bf16[512,128]{1,0:T(8,128)(2,1)S(1)}, bf16[512,128]{1,0:T(8,128)(2,1)}, u32[]{:S(2)}) copy-start(bf16[512,128]{1,0:T(8,128)(2,1)} %reshape.314) | copy-start | bytes 393220
  80.5 10.3 %all-to-all-start.7 = ((f32[8,64,128]{2,1,0:T(8,128)}), f32[8,64,128]{2,1,0:T(8,128)S(1)}, u32[]{:S(2)}, u32[]{:S(2)}) async-start(f32[8,64,128]{2,1,0:T(8,128)} %reshape.340), calls=%async_computation.7 | async-start | bytes 524288 | tf_op jit(solution)/shard_map/all_to_all | solution.py:203
  90.8 10.3 %all-to-all-start.8 = ((f32[8,64,128]{2,1,0:T(8,128)}), f32[8,64,128]{2,1,0:T(8,128)S(1)}, u32[]{:S(2)}, u32[]{:S(2)}) async-start(f32[8,64,128]{2,1,0:T(8,128)} %reshape.344), calls=%async_computation.8 | async-start | bytes 524288 | tf_op jit(solution)/shard_map/all_to_all | solution.py:204
  101.7 11.7 %collective-permute-start = (f32[2,32,512]{2,1,0:T(8,128)S(1)}, f32[2,32,512]{2,1,0:T(8,128)S(1)}, u32[]{:S(2)}, u32[]{:S(2)}) collective-permute-start(f32[2,32,512]{2,1,0:T(8,128)S(1)} %fusion.22), channel_id=1, source_target_pairs={{0,3},{4,7},{8,11},{12,15},{16,19},{20,23},{24,27},{28,31}} | collective-permute-start | bytes 393224 | tf_op jit(solution)/shard_map/ppermute | solution.py:22
  107.3 6.9 %collective-permute-start.1 = (f32[2,32,512]{2,1,0:T(8,128)S(1)}, f32[2,32,512]{2,1,0:T(8,128)S(1)}, u32[]{:S(2)}, u32[]{:S(2)}) collective-permute-start(f32[2,32,512]{2,1,0:T(8,128)S(1)} %fusion.22), channel_id=1, source_target_pairs={{1,0},{2,1},{3,2},{5,4},{6,5},{7,6},{9,8},{10,9},{11,10},{13,12},{... | collective-permute-start | bytes 393224 | tf_op jit(solution)/shard_map/ppermute | solution.py:22
  109.9 13.2 %all-to-all-start.6 = ((bf16[8,64,512]{2,1,0:T(8,128)(2,1)}), bf16[8,64,512]{2,1,0:T(8,128)(2,1)S(1)}, u32[]{:S(2)}, u32[]{:S(2)}) async-start(bf16[8,64,512]{2,1,0:T(8,128)(2,1)} %reshape.336), calls=%async_computation.6 | async-start | bytes 1048576 | tf_op jit(solution)/shard_map/all_to_all | solution.py:190
  114.1 9.2 %collective-permute-start.2 = (f32[2,32,512]{2,1,0:T(8,128)S(1)}, f32[2,32,512]{2,1,0:T(8,128)S(1)}, u32[]{:S(2)}, u32[]{:S(2)}) collective-permute-start(f32[2,32,512]{2,1,0:T(8,128)S(1)} %fusion.24), channel_id=1, source_target_pairs={{0,3},{4,7},{8,11},{12,15},{16,19},{20,23},{24,27},{28,31}} | collective-permute-start | bytes 393224 | tf_op jit(solution)/shard_map/ppermute | solution.py:22
  115.9 7.4 %collective-permute-start.3 = (f32[2,32,512]{2,1,0:T(8,128)S(1)}, f32[2,32,512]{2,1,0:T(8,128)S(1)}, u32[]{:S(2)}, u32[]{:S(2)}) collective-permute-start(f32[2,32,512]{2,1,0:T(8,128)S(1)} %fusion.24), channel_id=1, source_target_pairs={{1,0},{2,1},{3,2},{5,4},{6,5},{7,6},{9,8},{10,9},{11,10},{13,12},{... | collective-permute-start | bytes 393224 | tf_op jit(solution)/shard_map/ppermute | solution.py:22
  123.4 4.4 %collective-permute-start.4 = (f32[2,32,512]{2,1,0:T(8,128)S(1)}, f32[2,32,512]{2,1,0:T(8,128)S(1)}, u32[]{:S(2)}, u32[]{:S(2)}) collective-permute-start(f32[2,32,512]{2,1,0:T(8,128)S(1)} %fusion.26), channel_id=1, source_target_pairs={{0,3},{4,7},{8,11},{12,15},{16,19},{20,23},{24,27},{28,31}} | collective-permute-start | bytes 393224 | tf_op jit(solution)/shard_map/ppermute | solution.py:22
  125.1 6.9 %collective-permute-start.5 = (f32[2,32,512]{2,1,0:T(8,128)S(1)}, f32[2,32,512]{2,1,0:T(8,128)S(1)}, u32[]{:S(2)}, u32[]{:S(2)}) collective-permute-start(f32[2,32,512]{2,1,0:T(8,128)S(1)} %fusion.26), channel_id=1, source_target_pairs={{1,0},{2,1},{3,2},{5,4},{6,5},{7,6},{9,8},{10,9},{11,10},{13,12},{... | collective-permute-start | bytes 393224 | tf_op jit(solution)/shard_map/ppermute | solution.py:22
where the time goes:
time: 134 us; the launch traced here: 133 us
  starting transfers between devices  46.6 us (35%)
  waiting for transfers between devices  45.2 us (34%)
  local copies, waits for them, and re-layouts  21.2 us (16%)
  matrix products  10.9 us (8%)
  other arithmetic  7.36 us (5%)
  between operations  1.42 us (1%)
    ppermute x6, starting transfers between devices, passed_along(): return lax.ppermute(value, axis, pairs)  12.9 us
    all_to_all x1, waiting for transfers between devices, local(): lax.all_to_all(send_rows(output_grad), 'seq', split_axis=0, concat_axis=0...  7.61 us
    all_to_all x1, waiting for transfers between devices, local(): lax.all_to_all(send_rows(query_rows), 'seq', split_axis=0, concat_axis=0,...  6.61 us
    all_to_all x1, waiting for transfers between devices, local(): lax.all_to_all(send_partial(value_part), 'seq', split_axis=0, concat_axis...  6.17 us
    all_to_all x1, waiting for transfers between devices, local(): lax.all_to_all(query_send, 'seq', split_axis=0, concat_axis=0, tiled=True)  5.79 us
    all_to_all x1, starting transfers between devices, local(): lax.all_to_all(send_stats(log_norm), 'seq', split_axis=0, concat_axis=0,...  5.2 us
    ppermute x6, waiting for transfers between devices, passed_along(): return lax.ppermute(value, axis, pairs)  4.85 us
    all_to_all x1, waiting for transfers between devices, local(): lax.all_to_all(send_blocks(key_head), 'seq', split_axis=0, concat_axis=0,...  4.48 us
  transfers between devices with their start and end apart: 15, of which 10 were waited for; matrix products, arithmetic and copies ran while one was open for 20% of the time, Pallas kernels for 0%

commit v1 on v0

--- a/solution.py
+++ b/solution.py
@@ -3,6 +3,8 @@
 import jax
 import jax.numpy as jnp
 from jax import lax
+from jax.experimental import pallas as pl
+from jax.experimental.pallas import tpu as pltpu
 from jax.sharding import PartitionSpec as P
 
 HD = 128
@@ -219,6 +221,366 @@
     return (query_out, summed[0], summed[1])
 
 
+BF = jnp.bfloat16
+F32 = jnp.float32
+I32 = jnp.int32
+
+
+def mm(a, b, ca=1, cb=0):
+    return lax.dot_general(a, b, (((ca,), (cb,)), ((), ())), preferred_element_type=F32)
+
+
+def iota(shape, dim):
+    return lax.broadcasted_iota(I32, shape, dim)
+
+
+def pieces(x, count):
+    out = []
+    for _ in range(count):
+        part = x.astype(BF)
+        out.append(part)
+        x = x - part.astype(F32)
+    return out
+
+
+def peer_chip(chip, k, chips):
+    out, bit = 0, 1
+    while bit < chips:
+        out = out + (((chip // bit) + (k // bit)) % 2) * bit
+        bit *= 2
+    return out
+
+
+def fused_kernel(
+    q_ref, k_ref, v_ref, g_ref, ln_ref, rd_ref, disp_ref, list_ref, start_ref,
+    dq_ref, dk_ref, dv_ref,
+    kv_buf, perm, spread, qs, gs, qst, gst, lnb, rdb, posb, lowb, kpos, dq_acc,
+    keep, x_snd, x_rcv, c_snd, c_rcv, z_snd, z_rcv, f_snd, f_rcv,
+    d_ss, d_rs, p_ss, p_rs, x_ss, x_rs, c_ss, c_rs, z_ss, z_rs, f_ss, f_rs,
+):
+    owners = lax.axis_size("seq")
+    members = lax.axis_size("head")
+    chips = owners // 2
+    tok = q_ref.shape[0]
+    heads = q_ref.shape[1] // HD
+    spans = disp_ref.shape[1]
+    slots = spans // owners
+    rows = slots * SPAN
+    kvc = NLIST // owners
+    keys = kvc * KVCH
+    blocks = tok // KVCH
+    lanes = 2 * keys
+    shard = HD // members
+    scale = 1.0 / math.sqrt(HD)
+    me = lax.axis_index("seq")
+    z = lax.axis_index("head")
+    core = me % 2
+    other = 1 - core
+    chip = me // 2
+    partner = chip * 2 + other
+    near = [None] + [peer_chip(chip, k, chips) * 2 + core for k in range(1, chips)]
+
+    def remote(src, dst, ss, rs, seq, head):
+        return pltpu.make_async_remote_copy(
+            src_ref=src, dst_ref=dst, send_sem=ss, recv_sem=rs,
+            device_id={"seq": seq, "head": head}, device_id_type=pl.DeviceIdType.MESH,
+        )
+
+    barrier = pltpu.get_barrier_semaphore()
+    greet = [(partner, z)] + [(near[k], z) for k in range(1, chips)]
+    greet += [(me, (z + j) % members) for j in range(1, members)]
+    for seq, head in greet:
+        pl.semaphore_signal(
+            barrier, inc=1, device_id={"seq": seq, "head": head},
+            device_id_type=pl.DeviceIdType.MESH,
+        )
+
+    listed = list_ref[...].astype(F32)
+
+    def picks(home):
+        low = (home * blocks).astype(F32)
+        mine = (listed >= low) & (listed < low + blocks)
+        out, last = [], None
+        for r in range(kvc):
+            ok = mine if last is None else mine & (listed > last)
+            last = jnp.min(jnp.where(ok, listed, 1e9), axis=1, keepdims=True)
+            out.append(last)
+        return out
+
+    def make_spread(home, slot):
+        got = picks(home)
+        ahead = iota((KVCH, tok), 1) - iota((KVCH, tok), 0)
+        for g in range(owners):
+            for r in range(kvc):
+                at = ((got[r][g:g + 1, :] - (home * blocks).astype(F32)) * KVCH).astype(I32)
+                hot = jnp.where(ahead == at, 1.0, 0.0).astype(BF)
+                base = g * keys + r * KVCH
+                spread[slot, base:base + KVCH, :] = hot
+
+    make_spread(me, core)
+    kv_buf[0, core, :, 0:HD] = mm(spread[core], k_ref[...]).astype(BF)
+    kv_buf[0, core, :, HD:2 * HD] = mm(spread[core], v_ref[...]).astype(BF)
+    pl.semaphore_wait(barrier, len(greet))
+
+    mine0 = kv_buf.at[0, core]
+    direct, forward = {}, {}
+    for k in range(1, chips):
+        direct[k] = remote(mine0, kv_buf.at[k, core], d_ss.at[k], d_rs.at[k], near[k], z)
+        direct[k].start()
+    forward[0] = remote(mine0, mine0, p_ss.at[0], p_rs.at[0], partner, z)
+    forward[0].start()
+
+    make_spread(partner, other)
+    for k in range(chips):
+        lane = iota((owners, lanes), 1)
+        value = jnp.zeros((owners, lanes), I32)
+        for c in range(2):
+            for r, got in enumerate(picks(peer_chip(chip, k, chips) * 2 + c)):
+                block = c * kvc + r
+                inside = (lane >= block * KVCH) & (lane < (block + 1) * KVCH)
+                value = jnp.where(inside, (got * KVCH).astype(I32) + lane - block * KVCH, value)
+        for g in range(owners):
+            kpos[k, g] = value[g:g + 1, :]
+
+    def my_row(ref):
+        at = iota((owners, spans), 0) == me
+        return jnp.sum(jnp.where(at, ref[...].astype(F32), 0.0), axis=0, keepdims=True)
+
+    groups = my_row(disp_ref)
+    eye = iota((spans, spans), 0) == iota((spans, spans), 1)
+    column = jnp.sum(jnp.where(eye, groups, 0.0), axis=1, keepdims=True)
+    earlier = iota((spans, spans), 0) < iota((spans, spans), 1)
+    rank = jnp.sum(jnp.where((column == groups) & earlier, 1.0, 0.0), axis=0, keepdims=True)
+    dest = groups * slots + rank
+    starts = my_row(start_ref)
+    start_hi = jnp.floor(starts * (1.0 / 256.0))
+    start_lo = starts - start_hi * 256.0
+    fill = jnp.zeros((5, spans), F32)
+    small = jnp.concatenate([dest, start_hi, start_lo, fill], axis=0).astype(BF)
+    behind = iota((spans, tok), 1) - iota((spans, tok), 0) * SPAN
+    expand = jnp.where((behind >= 0) & (behind < SPAN), 1.0, 0.0).astype(BF)
+    wide = mm(small, expand)
+    token = iota((1, tok), 1)
+    span_of = jnp.floor((token.astype(F32) + 0.5) * (1.0 / SPAN))
+    within = token.astype(F32) - span_of * SPAN
+    target = (wide[0:1, :] * SPAN + within).astype(I32)
+    perm[...] = jnp.where(iota((tok, tok), 0) == target, 1.0, 0.0).astype(BF)
+
+    parts = pieces(ln_ref[...], 3) + pieces(rd_ref[...], 3)
+    parts += [wide[1:3, :].astype(BF), span_of.astype(BF)]
+    parts.append(jnp.zeros((1, tok), BF))
+    stats = jnp.concatenate([p.astype(F32) for p in parts], axis=0).astype(BF)
+    placed = mm(perm[...], stats, 1, 1)
+    hq = heads
+    norm = placed[:, 0:hq] + placed[:, hq:2 * hq] + placed[:, 2 * hq:3 * hq]
+    delta = placed[:, 3 * hq:4 * hq] + placed[:, 4 * hq:5 * hq] + placed[:, 5 * hq:6 * hq]
+    low = placed[:, 6 * hq:6 * hq + 1] * 256.0 + placed[:, 6 * hq + 1:6 * hq + 2]
+    slot_row = iota((tok, 1), 0).astype(F32)
+    slot_in = slot_row - jnp.floor((slot_row + 0.5) * (1.0 / SPAN)) * SPAN
+    pos = (placed[:, 6 * hq + 2:6 * hq + 3] + (me * spans).astype(F32)) * SPAN + slot_in
+    posb[...] = jnp.broadcast_to(pos.astype(I32), (tok, lanes)).reshape(owners, rows, lanes)
+    lowb[...] = jnp.broadcast_to(low.astype(I32), (tok, lanes)).reshape(owners, rows, lanes)
+    q_slot = mm(perm[...], q_ref[...]).astype(BF)
+    g_slot = mm(perm[...], g_ref[...]).astype(BF)
+    for g in range(owners):
+        at = slice(g * rows, (g + 1) * rows)
+        for h in range(heads):
+            to = slice(h * rows, (h + 1) * rows)
+            qs[g, to, :] = q_slot[at, h * HD:(h + 1) * HD]
+            gs[g, to, :] = g_slot[at, h * HD:(h + 1) * HD]
+            lnb[g, to, :] = jnp.broadcast_to(norm[at, h:h + 1], (rows, lanes))
+            rdb[g, to, :] = jnp.broadcast_to(delta[at, h:h + 1], (rows, lanes))
+
+    def transposes(g, carry):
+        qst[g] = qs[g].T
+        gst[g] = gs[g].T
+        return carry
+
+    lax.fori_loop(0, owners, transposes, 0)
+    is_first = core == 0
+
+    def compute(k):
+        def group(g, carry):
+            at = pl.ds(pl.multiple_of(g * keys, keys), keys)
+            key = jnp.concatenate([kv_buf[k, 0, at, 0:HD], kv_buf[k, 1, at, 0:HD]], axis=0)
+            val = jnp.concatenate(
+                [kv_buf[k, 0, at, HD:2 * HD], kv_buf[k, 1, at, HD:2 * HD]], axis=0
+            )
+            where_key = kpos[k, g]
+            allowed = (where_key <= posb[g]) & (where_key >= lowb[g])
+            allowed = jnp.concatenate([allowed] * heads, axis=0)
+            scores = mm(qs[g], key, 1, 1) * scale
+            probs = jnp.where(allowed, jnp.exp(scores - lnb[g]), 0.0)
+            dprobs = mm(gs[g], val, 1, 1)
+            dscores = probs * (dprobs - rdb[g])
+            probs_b = probs.astype(BF)
+            dscores_b = dscores.astype(BF)
+            dv = mm(gst[g], probs_b)
+            dk = mm(qst[g], dscores_b)
+            keep[k, g] = jnp.where(is_first, dk, dv)
+            x_snd[k, g] = jnp.where(is_first, dv, dk).astype(BF)
+            dq = mm(dscores_b, key)
+            if k == 0:
+                dq_acc[g] = dq
+            else:
+                dq_acc[g] += dq
+            return carry
+
+        lax.fori_loop(0, owners, group, 0, unroll=2)
+
+    def pass_on(k):
+        direct[k].wait_recv()
+        block = kv_buf.at[k, core]
+        forward[k] = remote(block, block, p_ss.at[k], p_rs.at[k], partner, z)
+        forward[k].start()
+
+    swap, onward = {}, {}
+
+    def exchange(k):
+        swap[k] = remote(x_snd.at[k], x_rcv.at[k], x_ss.at[k], x_rs.at[k], partner, z)
+        swap[k].start()
+
+    def send_home(k):
+        swap[k].wait_recv()
+        c_snd[k] = (keep[k] + x_rcv[k].astype(F32)).astype(BF)
+        onward[k] = remote(c_snd.at[k], c_rcv.at[k], c_ss.at[k], c_rs.at[k], near[k], z)
+        onward[k].start()
+
+    forward[0].wait_recv()
+    compute(0)
+    exchange(0)
+    for k in range(1, min(3, chips)):
+        pass_on(k)
+    for k in range(1, chips):
+        if k >= 3:
+            pass_on(k)
+        forward[k].wait_recv()
+        compute(k)
+        exchange(k)
+        if k > 1:
+            send_home(k - 1)
+    if chips > 1:
+        send_home(chips - 1)
+
+    pulled = []
+    for h in range(heads):
+        to = slice(h * rows, (h + 1) * rows)
+        pulled.append(
+            jnp.concatenate([(dq_acc[g, to, :] * scale).astype(BF) for g in range(owners)], axis=0)
+        )
+    dq_ref[...] = mm(perm[...], jnp.concatenate(pulled, axis=1), 0, 0).astype(BF)
+
+    swap[0].wait_recv()
+    total = keep[0] + x_rcv[0].astype(F32)
+    for k in range(1, chips):
+        onward[k].wait_recv()
+        total = total + c_rcv[k].astype(F32)
+    keep[0] = total
+    z_snd[...] = total.astype(BF)
+    around = []
+    for j in range(1, members):
+        to = (z + j) % members
+        piece = z_snd.at[:, pl.ds(pl.multiple_of(to * shard, shard), shard), :]
+        copy = remote(piece, z_rcv.at[j], z_ss.at[j], z_rs.at[j], me, to)
+        copy.start()
+        around.append((j, copy))
+    block = keep[0, :, pl.ds(pl.multiple_of(z * shard, shard), shard), :]
+    for j, copy in around:
+        copy.wait_recv()
+        block = block + z_rcv[j].astype(F32)
+    block = block * jnp.where(is_first, scale, 1.0)
+    done = []
+    for c in range(2):
+        packed = jnp.concatenate([block[g][:, c * keys:(c + 1) * keys] for g in range(owners)], axis=1)
+        got = mm(jnp.concatenate(pieces(packed, 3), axis=0), spread[c])
+        done.append(got[0:shard] + got[shard:2 * shard] + got[2 * shard:3 * shard])
+    f_snd[...] = jnp.where(is_first, done[1], done[0])
+    last = remote(f_snd, f_rcv, f_ss, f_rs, partner, z)
+    last.start()
+    own = jnp.where(is_first, done[0], done[1])
+    last.wait_recv()
+    theirs = f_rcv[...]
+    dk_ref[...] = jnp.where(is_first, own, theirs)
+    dv_ref[...] = jnp.where(is_first, theirs, own)
+    for copy in list(direct.values()) + list(forward.values()) + list(swap.values()):
+        copy.wait_send()
+    for copy in list(onward.values()) + [copy for _, copy in around] + [last]:
+        copy.wait_send()
+
+
+def fused(query_rows, key_rows, value_rows, output_grad, log_norm, row_delta, dispatch, listed_spans, range_start):
+    owners = lax.axis_size("seq")
+    members = lax.axis_size("head")
+    chips = owners // 2
+    tok, width = query_rows.shape
+    heads = width // HD
+    rows = dispatch.shape[1] // owners * SPAN
+    keys = NLIST // owners * KVCH
+    lanes = 2 * keys
+    shard = HD // members
+    vm = pltpu.VMEM
+    dma = pltpu.SemaphoreType.DMA
+    scratch = [
+        vm((chips, 2, owners * keys, 2 * HD), BF),
+        vm((tok, tok), BF),
+        vm((2, owners * keys, tok), BF),
+        vm((owners, heads * rows, HD), BF),
+        vm((owners, heads * rows, HD), BF),
+        vm((owners, HD, heads * rows), BF),
+        vm((owners, HD, heads * rows), BF),
+        vm((owners, heads * rows, lanes), F32),
+        vm((owners, heads * rows, lanes), F32),
+        vm((owners, rows, lanes), I32),
+        vm((owners, rows, lanes), I32),
+        vm((chips, owners, 1, lanes), I32),
+        vm((owners, heads * rows, HD), F32),
+        vm((chips, owners, HD, lanes), F32),
+        vm((chips, owners, HD, lanes), BF),
+        vm((chips, owners, HD, lanes), BF),
+        vm((chips, owners, HD, lanes), BF),
+        vm((chips, owners, HD, lanes), BF),
+        vm((owners, HD, lanes), BF),
+        vm((members, owners, shard, lanes), BF),
+        vm((shard, tok), F32),
+        vm((shard, tok), F32),
+        dma((chips,)), dma((chips,)), dma((chips,)), dma((chips,)),
+        dma((chips,)), dma((chips,)), dma((chips,)), dma((chips,)),
+        dma((members,)), dma((members,)), dma, dma,
+    ]
+    spec = pl.BlockSpec(memory_space=pltpu.VMEM)
+    return pl.pallas_call(
+        fused_kernel,
+        out_shape=(
+            jax.ShapeDtypeStruct((tok, width), BF),
+            jax.ShapeDtypeStruct((shard, tok), F32),
+            jax.ShapeDtypeStruct((shard, tok), F32),
+        ),
+        in_specs=[spec] * 9,
+        out_specs=(spec, spec, spec),
+        scratch_shapes=scratch,
+        compiler_params=pltpu.CompilerParams(
+            collective_id=0, has_side_effects=True, vmem_limit_bytes=56 * 1024 * 1024
+        ),
+    )(query_rows, key_rows, value_rows, output_grad, log_norm, row_delta, dispatch, listed_spans, range_start)
+
+
+def step(*args):
+    query_rows, key_rows, dispatch = args[0], args[1], args[6]
+    owners = lax.axis_size("seq")
+    members = lax.axis_size("head")
+    heads = query_rows.shape[1] // HD
+    dense = (
+        owners % 2 == 0
+        and owners & (owners - 1) == 0
+        and NLIST % owners == 0
+        and 2 * NLIST // owners * KVCH == HD
+        and dispatch.shape[1] % owners == 0
+        and key_rows.shape[1] == HD
+        and members * heads == GROUP
+    )
+    return fused(*args) if dense else local(*args)
+
+
 def solution(mesh):
     placed = (
         P("seq", "head"),
@@ -232,7 +594,7 @@
         P(),
     )
     return jax.shard_map(
-        local,
+        step,
         mesh=mesh,
         in_specs=placed,
         out_specs=(P("seq", "head"), P("head", "seq"), P("head", "seq")),

time: 134 us -> 49.3 us (0.37)
  starting transfers between devices: 46.6 us -> 0 us
  waiting for transfers between devices: 45.2 us -> 0 us
  Pallas kernels: 0 us -> 45 us
  local copies, waits for them, and re-layouts: 21.2 us -> 3.4 us
  matrix products: 10.9 us -> 0 us
  other arithmetic: 7.36 us -> 0 us
    pallas_call x0 -> x1, Pallas kernels: none -> 45 us  [fused(): pl.pallas_call(fused_kernel, out_shape=(jax.ShapeDtypeStruct((tok, width)...]
    all_to_all x9 -> x0, waiting for transfers between devices: 40.4 us -> none  [the longest x1 7.61 us: local(): lax.all_to_all(send_rows(output_grad), 'seq', split_axis=0, concat_axis=0...]
    all_to_all x9 -> x0, starting transfers between devices: 33.6 us -> none  [the longest x1 5.2 us: local(): lax.all_to_all(send_stats(log_norm), 'seq', split_axis=0, concat_axis=0,...]
    reshape x40 -> x0, local copies, waits for them, and re-layouts: 14 us -> none  [the longest x2 2.57 us: send_rows(): rows.reshape(spans, -1)]
    ppermute x6 -> x0, starting transfers between devices: 12.9 us -> none  [passed_along(): return lax.ppermute(value, axis, pairs)]
    dot_general x25 -> x0, matrix products: 10.9 us -> none  [the longest x1 2.55 us: local(): jnp.einsum('qhd,kd->hqk', grad_mine, value_mine, preferred_element_type=j...]
    ppermute x6 -> x0, waiting for transfers between devices: 4.85 us -> none  [passed_along(): return lax.ppermute(value, axis, pairs)]
    unnamed x16 -> x7, local copies, waits for them, and re-layouts: 1.58 us -> 3.4 us
  transfers between devices with their start and end apart: 15 -> 0, of which waited for: 10 -> 0; matrix products, arithmetic and copies ran while one was open for 20% -> 0% of each run, Pallas kernels for 0% -> 0%
where the time goes in v1:
time: 49.3 us; the launch traced here: 49.1 us
  Pallas kernels  45 us (91%)
  local copies, waits for them, and re-layouts  3.4 us (7%)
  between operations  0.65 us (1%)
    pallas_call x1, Pallas kernels, fused(): pl.pallas_call(fused_kernel, out_shape=(jax.ShapeDtypeStruct((tok, width)...  45 us
    unnamed x7, local copies, waits for them, and re-layouts  3.4 us

profile of v1, /device:TPU:0, one launch (start us, length us, event | category | flops | bytes accessed | tf_op | source)
XLA Modules:
  0.0 49.1 jit_solution(13328090691118144758)
XLA Ops:
  0.6 45.0 %shard_map.112 = (bf16[512,512]{1,0:T(8,128)(2,1)}, f32[32,512]{1,0:T(8,128)}, f32[32,512]{1,0:T(8,128)}) custom-call(bf16[512,512]{1,0:T(8,128)(2,1)} %q_ref.1, bf16[512,128]{1,0:T(8,128)(2,1)} %k_ref.1, bf16[512,128]{1,0:T(8,128)(2,1)} %v_ref.1, bf16[512,512]{1,0:T(8,128)(2,1)} %g_ref.1, f32[4,512]{1,0:T(4,128)} %ln_ref.1, f32[4,512]{1,0:T(4,128)} %rd_ref.1, ...), custom_call_target="tpu_custom_call" | custom-call | tf_op jit(solution)/shard_map/pallas_call | solution.py:551
  45.7 0.0 copy-start.1
  45.7 1.9 %copy.15 = bf16[512,512]{1,0:T(8,128)(2,1)} copy(bf16[512,512]{1,0:T(8,128)(2,1)} %get-tuple-element.6) | data formatting | bytes 1048576
  47.6 0.0 copy-done.1
  47.6 0.0 copy-start
  47.6 0.6 %copy.16 = f32[32,512]{1,0:T(8,128)} copy(f32[32,512]{1,0:T(8,128)S(1)} %copy-done.1) | data formatting | bytes 131072
  48.2 0.2 copy-done
  48.5 0.6 %copy.17 = f32[32,512]{1,0:T(8,128)} copy(f32[32,512]{1,0:T(8,128)S(1)} %copy-done) | data formatting | bytes 131072
Async XLA Ops:
  45.7 1.9 %copy-start.1 = (f32[32,512]{1,0:T(8,128)S(1)}, f32[32,512]{1,0:T(8,128)}, u32[]{:S(2)}) copy-start(f32[32,512]{1,0:T(8,128)} %get-tuple-element.7) | copy-start | bytes 196612
  47.6 0.9 %copy-start = (f32[32,512]{1,0:T(8,128)S(1)}, f32[32,512]{1,0:T(8,128)}, u32[]{:S(2)}) copy-start(f32[32,512]{1,0:T(8,128)} %get-tuple-element.8) | copy-start | bytes 196612

commit v2 on v1

--- a/solution.py
+++ b/solution.py
@@ -226,6 +226,11 @@
 I32 = jnp.int32
 
 
+CHUNKS = 2
+CHIPS = 4
+FIRST = 0
+
+
 def mm(a, b, ca=1, cb=0):
     return lax.dot_general(a, b, (((ca,), (cb,)), ((), ())), preferred_element_type=F32)
 
@@ -256,7 +261,8 @@
     dq_ref, dk_ref, dv_ref,
     kv_buf, perm, spread, qs, gs, qst, gst, lnb, rdb, posb, lowb, kpos, dq_acc,
     keep, x_snd, x_rcv, c_snd, c_rcv, z_snd, z_rcv, f_snd, f_rcv,
-    d_ss, d_rs, p_ss, p_rs, x_ss, x_rs, c_ss, c_rs, z_ss, z_rs, f_ss, f_rs,
+    q_in, g_in, dq_out,
+    d_ss, d_rs, p_ss, p_rs, x_ss, x_rs, c_ss, c_rs, z_ss, z_rs, f_ss, f_rs, l_sem,
 ):
     owners = lax.axis_size("seq")
     members = lax.axis_size("head")
@@ -264,6 +270,12 @@
     tok = q_ref.shape[0]
     heads = q_ref.shape[1] // HD
     spans = disp_ref.shape[1]
+    chunks = d_ss.shape[1]
+    width = owners // chunks
+    load_q = pltpu.make_async_copy(q_ref, q_in, l_sem.at[0])
+    load_g = pltpu.make_async_copy(g_ref, g_in, l_sem.at[1])
+    load_q.start()
+    load_g.start()
     slots = spans // owners
     rows = slots * SPAN
     kvc = NLIST // owners
@@ -322,13 +334,27 @@
     kv_buf[0, core, :, HD:2 * HD] = mm(spread[core], v_ref[...]).astype(BF)
     pl.semaphore_wait(barrier, len(greet))
 
-    mine0 = kv_buf.at[0, core]
-    direct, forward = {}, {}
+    direct, forward, across = {}, {}, {}
+    beside = z + 1 - 2 * (z % 2)
+
+    def turn(c):
+        return (c + z) % chunks
+
+    def part(k, c):
+        at = pl.multiple_of(turn(c) * width * keys, width * keys)
+        return kv_buf.at[k, core, pl.ds(at, width * keys)]
+
+    def to_partner(k, c):
+        at = (k, turn(c))
+        forward[k, c] = remote(part(k, c), part(k, c), p_ss.at[at], p_rs.at[at], partner, z)
+        forward[k, c].start()
+
     for k in range(1, chips):
-        direct[k] = remote(mine0, kv_buf.at[k, core], d_ss.at[k], d_rs.at[k], near[k], z)
+        at = (k, turn(0))
+        direct[k] = remote(part(0, 0), part(k, 0), d_ss.at[at], d_rs.at[at], near[k], z)
         direct[k].start()
-    forward[0] = remote(mine0, mine0, p_ss.at[0], p_rs.at[0], partner, z)
-    forward[0].start()
+    for c in range(chunks):
+        to_partner(0, c)
 
     make_spread(partner, other)
     for k in range(chips):
@@ -380,8 +406,10 @@
     pos = (placed[:, 6 * hq + 2:6 * hq + 3] + (me * spans).astype(F32)) * SPAN + slot_in
     posb[...] = jnp.broadcast_to(pos.astype(I32), (tok, lanes)).reshape(owners, rows, lanes)
     lowb[...] = jnp.broadcast_to(low.astype(I32), (tok, lanes)).reshape(owners, rows, lanes)
-    q_slot = mm(perm[...], q_ref[...]).astype(BF)
-    g_slot = mm(perm[...], g_ref[...]).astype(BF)
+    load_q.wait()
+    q_slot = mm(perm[...], q_in[...]).astype(BF)
+    load_g.wait()
+    g_slot = mm(perm[...], g_in[...]).astype(BF)
     for g in range(owners):
         at = slice(g * rows, (g + 1) * rows)
         for h in range(heads):
@@ -399,8 +427,9 @@
     lax.fori_loop(0, owners, transposes, 0)
     is_first = core == 0
 
-    def compute(k):
-        def group(g, carry):
+    def compute(k, c):
+        def group(i, carry):
+            g = turn(c) * width + i
             at = pl.ds(pl.multiple_of(g * keys, keys), keys)
             key = jnp.concatenate([kv_buf[k, 0, at, 0:HD], kv_buf[k, 1, at, 0:HD]], axis=0)
             val = jnp.concatenate(
@@ -420,80 +449,119 @@
             keep[k, g] = jnp.where(is_first, dk, dv)
             x_snd[k, g] = jnp.where(is_first, dv, dk).astype(BF)
             dq = mm(dscores_b, key)
-            if k == 0:
+            if k == FIRST:
                 dq_acc[g] = dq
             else:
                 dq_acc[g] += dq
             return carry
 
-        lax.fori_loop(0, owners, group, 0, unroll=2)
-
-    def pass_on(k):
+        lax.fori_loop(0, width, group, 0, unroll=min(width, 4))
+        exchange(k, c)
+
+    swap, onward, around = {}, {}, {}
+
+    def those(c):
+        return pl.ds(turn(c) * width, width)
+
+    def exchange(k, c):
+        swap[k, c] = remote(
+            x_snd.at[k, those(c)], x_rcv.at[k, those(c)], x_ss.at[k, turn(c)], x_rs.at[k, turn(c)], partner, z
+        )
+        swap[k, c].start()
+
+    def send_home(k, c):
+        swap[k, c].wait_recv()
+        c_snd[k, those(c)] = (keep[k, those(c)] + x_rcv[k, those(c)].astype(F32)).astype(BF)
+        onward[k, c] = remote(
+            c_snd.at[k, those(c)], c_rcv.at[k, those(c)], c_ss.at[k, turn(c)], c_rs.at[k, turn(c)], near[k], z
+        )
+        onward[k, c].start()
+
+    def pass_first(k):
         direct[k].wait_recv()
-        block = kv_buf.at[k, core]
-        forward[k] = remote(block, block, p_ss.at[k], p_rs.at[k], partner, z)
-        forward[k].start()
-
-    swap, onward = {}, {}
-
-    def exchange(k):
-        swap[k] = remote(x_snd.at[k], x_rcv.at[k], x_ss.at[k], x_rs.at[k], partner, z)
-        swap[k].start()
-
-    def send_home(k):
-        swap[k].wait_recv()
-        c_snd[k] = (keep[k] + x_rcv[k].astype(F32)).astype(BF)
-        onward[k] = remote(c_snd.at[k], c_rcv.at[k], c_ss.at[k], c_rs.at[k], near[k], z)
-        onward[k].start()
-
-    forward[0].wait_recv()
-    compute(0)
-    exchange(0)
-    for k in range(1, min(3, chips)):
-        pass_on(k)
-    for k in range(1, chips):
-        if k >= 3:
-            pass_on(k)
-        forward[k].wait_recv()
-        compute(k)
-        exchange(k)
-        if k > 1:
-            send_home(k - 1)
-    if chips > 1:
-        send_home(chips - 1)
-
+        across[k] = remote(
+            part(k, 0), part(k, 0), d_ss.at[k, turn(1)], d_rs.at[k, turn(0)], me, beside
+        )
+        across[k].start()
+        to_partner(k, 0)
+
+    def pass_second(k):
+        remote(
+            part(k, 1), part(k, 1), d_ss.at[k, turn(1)], d_rs.at[k, turn(1)], me, beside
+        ).wait_recv()
+        to_partner(k, 1)
+
+    def work(k, c):
+        forward[k, c].wait_recv()
+        compute(k, c)
+
+    def total_up(c):
+        swap[0, c].wait_recv()
+        total = keep[0, those(c)] + x_rcv[0, those(c)].astype(F32)
+        for k in range(1, chips):
+            onward[k, c].wait_recv()
+            total = total + c_rcv[k, those(c)].astype(F32)
+        keep[0, those(c)] = total
+        z_snd[those(c)] = total.astype(BF)
+        for j in range(1, members):
+            to = (z + j) % members
+            piece = z_snd.at[those(c), pl.ds(pl.multiple_of(to * shard, shard), shard), :]
+            around[j, c] = remote(
+                piece, z_rcv.at[j, those(c)], z_ss.at[j, turn(c)], z_rs.at[j, turn(c)], me, to
+            )
+            around[j, c].start()
+
+    done = [None, None]
+
+    def settle(c):
+        block = keep[0, those(c), pl.ds(pl.multiple_of(z * shard, shard), shard), :]
+        for j in range(1, members):
+            around[j, c].wait_recv()
+            block = block + z_rcv[j, those(c)].astype(F32)
+        block = block * jnp.where(is_first, scale, 1.0)
+        base = pl.multiple_of(turn(c) * width * keys, width * keys)
+        for side in range(2):
+            packed = jnp.concatenate(
+                [block[i][:, side * keys:(side + 1) * keys] for i in range(width)], axis=1
+            )
+            hot = spread[side, pl.ds(base, width * keys), :]
+            got = mm(jnp.concatenate(pieces(packed, 2), axis=0), hot)
+            got = got[0:shard] + got[shard:2 * shard]
+            done[side] = got if done[side] is None else done[side] + got
+
+    work(0, 0)
+    pass_first(1)
+    pass_first(2)
+    work(1, 0)
+    pass_first(3)
+    work(2, 0)
+    send_home(1, 0)
+    work(3, 0)
+    send_home(2, 0)
+    pass_second(1)
+    work(0, 1)
+    send_home(3, 0)
+    work(1, 1)
+    pass_second(2)
+    send_home(1, 1)
+    work(2, 1)
+    pass_second(3)
+    send_home(2, 1)
+    work(3, 1)
+    send_home(chips - 1, 1)
     pulled = []
     for h in range(heads):
         to = slice(h * rows, (h + 1) * rows)
         pulled.append(
             jnp.concatenate([(dq_acc[g, to, :] * scale).astype(BF) for g in range(owners)], axis=0)
         )
-    dq_ref[...] = mm(perm[...], jnp.concatenate(pulled, axis=1), 0, 0).astype(BF)
-
-    swap[0].wait_recv()
-    total = keep[0] + x_rcv[0].astype(F32)
-    for k in range(1, chips):
-        onward[k].wait_recv()
-        total = total + c_rcv[k].astype(F32)
-    keep[0] = total
-    z_snd[...] = total.astype(BF)
-    around = []
-    for j in range(1, members):
-        to = (z + j) % members
-        piece = z_snd.at[:, pl.ds(pl.multiple_of(to * shard, shard), shard), :]
-        copy = remote(piece, z_rcv.at[j], z_ss.at[j], z_rs.at[j], me, to)
-        copy.start()
-        around.append((j, copy))
-    block = keep[0, :, pl.ds(pl.multiple_of(z * shard, shard), shard), :]
-    for j, copy in around:
-        copy.wait_recv()
-        block = block + z_rcv[j].astype(F32)
-    block = block * jnp.where(is_first, scale, 1.0)
-    done = []
-    for c in range(2):
-        packed = jnp.concatenate([block[g][:, c * keys:(c + 1) * keys] for g in range(owners)], axis=1)
-        got = mm(jnp.concatenate(pieces(packed, 3), axis=0), spread[c])
-        done.append(got[0:shard] + got[shard:2 * shard] + got[2 * shard:3 * shard])
+    dq_out[...] = mm(perm[...], jnp.concatenate(pulled, axis=1), 0, 0).astype(BF)
+    save = pltpu.make_async_copy(dq_out, dq_ref, l_sem.at[2])
+    save.start()
+    total_up(0)
+    total_up(1)
+    for c in range(chunks):
+        settle(c)
     f_snd[...] = jnp.where(is_first, done[1], done[0])
     last = remote(f_snd, f_rcv, f_ss, f_rs, partner, z)
     last.start()
@@ -502,10 +570,32 @@
     theirs = f_rcv[...]
     dk_ref[...] = jnp.where(is_first, own, theirs)
     dv_ref[...] = jnp.where(is_first, theirs, own)
-    for copy in list(direct.values()) + list(forward.values()) + list(swap.values()):
-        copy.wait_send()
-    for copy in list(onward.values()) + [copy for _, copy in around] + [last]:
-        copy.wait_send()
+    for made in (direct, forward, across, swap, onward, around):
+        for copy in made.values():
+            copy.wait_send()
+    last.wait_send()
+    save.wait()
+
+
+def place_kernel(a_ref, b_ref, c_ref, x_ref, y_ref, w_ref, sems):
+    pairs = ((a_ref, x_ref), (b_ref, y_ref), (c_ref, w_ref))
+    moves = [pltpu.make_async_copy(a, b, sems.at[i]) for i, (a, b) in enumerate(pairs)]
+    for move in moves:
+        move.start()
+    for move in moves:
+        move.wait()
+
+
+def place(outs):
+    spec = pl.BlockSpec(memory_space=pltpu.VMEM)
+    far = pl.BlockSpec(memory_space=pl.ANY)
+    return pl.pallas_call(
+        place_kernel,
+        out_shape=tuple(jax.ShapeDtypeStruct(o.shape, o.dtype) for o in outs),
+        in_specs=[spec] * 3,
+        out_specs=(far,) * 3,
+        scratch_shapes=[pltpu.SemaphoreType.DMA((3,))],
+    )(*outs)
 
 
 def fused(query_rows, key_rows, value_rows, output_grad, log_norm, row_delta, dispatch, listed_spans, range_start):
@@ -518,6 +608,7 @@
     keys = NLIST // owners * KVCH
     lanes = 2 * keys
     shard = HD // members
+    chunks = CHUNKS
     vm = pltpu.VMEM
     dma = pltpu.SemaphoreType.DMA
     scratch = [
@@ -543,11 +634,15 @@
         vm((members, owners, shard, lanes), BF),
         vm((shard, tok), F32),
         vm((shard, tok), F32),
-        dma((chips,)), dma((chips,)), dma((chips,)), dma((chips,)),
-        dma((chips,)), dma((chips,)), dma((chips,)), dma((chips,)),
-        dma((members,)), dma((members,)), dma, dma,
+        vm((tok, width), BF),
+        vm((tok, width), BF),
+        vm((tok, width), BF),
+        dma((chips, chunks)), dma((chips, chunks)), dma((chips, chunks)), dma((chips, chunks)),
+        dma((chips, chunks)), dma((chips, chunks)), dma((chips, chunks)), dma((chips, chunks)),
+        dma((members, chunks)), dma((members, chunks)), dma, dma, dma((3,)),
     ]
     spec = pl.BlockSpec(memory_space=pltpu.VMEM)
+    far = pl.BlockSpec(memory_space=pl.ANY)
     return pl.pallas_call(
         fused_kernel,
         out_shape=(
@@ -555,8 +650,8 @@
             jax.ShapeDtypeStruct((shard, tok), F32),
             jax.ShapeDtypeStruct((shard, tok), F32),
         ),
-        in_specs=[spec] * 9,
-        out_specs=(spec, spec, spec),
+        in_specs=[far, spec, spec, far] + [spec] * 5,
+        out_specs=(far, spec, spec),
         scratch_shapes=scratch,
         compiler_params=pltpu.CompilerParams(
             collective_id=0, has_side_effects=True, vmem_limit_bytes=56 * 1024 * 1024
@@ -570,15 +665,15 @@
     members = lax.axis_size("head")
     heads = query_rows.shape[1] // HD
     dense = (
-        owners % 2 == 0
-        and owners & (owners - 1) == 0
+        owners // 2 == CHIPS
+        and members % CHUNKS == 0
         and NLIST % owners == 0
         and 2 * NLIST // owners * KVCH == HD
         and dispatch.shape[1] % owners == 0
         and key_rows.shape[1] == HD
         and members * heads == GROUP
     )
-    return fused(*args) if dense else local(*args)
+    return place(fused(*args)) if dense else local(*args)
 
 
 def solution(mesh):

time: 49.3 us -> 39.8 us (0.81)
  Pallas kernels: 45 us -> 39 us
  local copies, waits for them, and re-layouts: 3.4 us -> 0 us
    pallas_call x1, Pallas kernels: 45 us -> 37 us  [fused(): pl.pallas_call(fused_kernel, out_shape=(jax.ShapeDtypeStruct((tok, width)...]
    unnamed x7 -> x0, local copies, waits for them, and re-layouts: 3.4 us -> none
    pallas_call x0 -> x1, Pallas kernels: none -> 1.93 us  [place(): pl.pallas_call(place_kernel, out_shape=tuple((jax.ShapeDtypeStruct(o.shap...]
where the time goes in v2:
time: 39.8 us; the launch traced here: 39.6 us
  Pallas kernels  39 us (98%)
  between operations  0.64 us (2%)
    pallas_call x1, Pallas kernels, fused(): pl.pallas_call(fused_kernel, out_shape=(jax.ShapeDtypeStruct((tok, width)...  37 us
    pallas_call x1, Pallas kernels, place(): pl.pallas_call(place_kernel, out_shape=tuple((jax.ShapeDtypeStruct(o.shap...  1.93 us

profile of v2, /device:TPU:0, one launch (start us, length us, event | category | flops | bytes accessed | tf_op | source)
XLA Modules:
  0.0 39.6 jit_solution(10905086089364226407)
XLA Ops:
  0.6 37.0 %shard_map.112 = (bf16[512,512]{1,0:T(8,128)(2,1)}, f32[32,512]{1,0:T(8,128)}, f32[32,512]{1,0:T(8,128)}) custom-call(bf16[512,512]{1,0:T(8,128)(2,1)} %q_ref.1, bf16[512,128]{1,0:T(8,128)(2,1)} %k_ref.1, bf16[512,128]{1,0:T(8,128)(2,1)} %v_ref.1, bf16[512,512]{1,0:T(8,128)(2,1)} %g_ref.1, f32[4,512]{1,0:T(4,128)} %ln_ref.1, f32[4,512]{1,0:T(4,128)} %rd_ref.1, ...), custom_call_target="tpu_custom_call" | custom-call | tf_op jit(solution)/shard_map/pallas_call | solution.py:646
  37.7 1.9 %shard_map.113 = (bf16[512,512]{1,0:T(8,128)(2,1)}, f32[32,512]{1,0:T(8,128)}, f32[32,512]{1,0:T(8,128)}) custom-call(bf16[512,512]{1,0:T(8,128)(2,1)} %get-tuple-element.6.a_ref, f32[32,512]{1,0:T(8,128)} %get-tuple-element.7.b_ref, f32[32,512]{1,0:T(8,128)} %get-tuple-element.8.c_ref), custom_call_target="tpu_custom_call" | custom-call | tf_op jit(solution)/shard_map/pallas_call | solution.py:592
